TPU v7x, 256 devices: a whole 4x4x8 slice. The times are simulated.
256 devices in a mesh: expert: 64 (over y, x, z_lo), dp: 4 (over z_hi, core).
Axes of the slice: x: 4, y: 4, z: 8 (z_hi: 2, z_lo: 4; z = z_hi * 4 + z_lo), core: 2. Of those that a mesh axis runs over, the one named last changes fastest.
Arguments:
- tokens: bfloat16 [3072, 3584], P('expert'), may hold values from -6 to 6
- expert_weights: bfloat16 [64, 3, 3584, 1024], P('expert', None, None, 'dp'), may hold values from -0.09375 to 0.09375
- partner: int32 [64], replicated, may hold values from 0 to 63, as said below
- replica: int32 [64], replicated, may hold values from 0 to 63, as said below
- routing: int32 [3072, 8], P('expert'), may hold values from 0 to 127, all different within a row; in each aligned block of 48 rows (0 to 47, 48 to 95, ...) at most 6 rows name the same one
- gates: bfloat16 [3072, 8], P('expert'), may hold values from 0.099609375 to 1
Outputs:
- mixed: bfloat16 [3072, 3584], P('expert', 'dp')
Inputs may be any that keep to these rules, and one draw needn't show every extreme that they name: partner pairs devices: partner[partner[p]] = p; about half of the indices are paired with another, the rest with themselves. No expert appears more than 4 times in replica, and some expert appears exactly 4 times. `routing`: each row names 8 different slots; among the 48 rows of one device along expert no slot is named more than 6 times.
All inputs are finite; a program needn't handle non-finite values.
Results may differ from a plain program's by a relative error of at most 0.0058.
Values may be sent and summed in bfloat16 or wider, within the bound.
A program may use at most 128 MiB of HBM per device.

v0:
```python
import jax
import jax.numpy as jnp
from jax import lax
from jax.sharding import Mesh, PartitionSpec as P

GATHER_AXES = ("z_lo", "y", "x")
OWNER = ("y", "x", "z_lo")


def expert_hidden(packed, features, topk, hit, w):
    x = packed[:, :features]
    slots = packed[:, features : features + topk].astype(jnp.float32)
    weight = packed[:, features + topk : features + 2 * topk].astype(jnp.float32)
    ids = jnp.arange(hit.shape[0], dtype=jnp.float32)
    sel = jnp.sum(jnp.where((slots[:, :, None] == ids) & hit, weight[:, :, None], 0.0), axis=(1, 2))
    g = jnp.dot(x, w[0], preferred_element_type=jnp.float32)
    u = jnp.dot(x, w[1], preferred_element_type=jnp.float32)
    return ((jax.nn.silu(g) * u).astype(jnp.bfloat16), sel)


def down_project(h, sel, w_down):
    down = lax.dot_general(h, w_down, (((1,), (1,)), ((), ())), preferred_element_type=jnp.float32)
    return down * sel[:, None]


def shards(tokens, expert_weights, partner, replica, routing, gates):
    rows, features = tokens.shape
    topk = routing.shape[1]
    me = lax.axis_index(OWNER)
    core = lax.axis_index("core")
    half = rows // 2
    packed = jnp.concatenate(
        [
            tokens,
            routing.astype(jnp.bfloat16),
            gates,
            jnp.zeros((rows, 128 - 2 * topk), jnp.bfloat16),
        ],
        axis=1,
    )
    own = lax.dynamic_slice_in_dim(packed, core * half, half, axis=0)
    for axis in GATHER_AXES:
        own = lax.all_gather(own, axis, axis=0, tiled=True)
    other = lax.ppermute(own, "core", [(0, 1), (1, 0)])
    hit = jnp.stack([partner, replica], axis=1).reshape(-1) == me
    w = expert_weights[0]
    h_own, sel_own = expert_hidden(own, features, topk, hit, w)
    h_other, sel_other = expert_hidden(other, features, topk, hit, w)
    away = down_project(h_other, sel_other, w[2]).astype(jnp.bfloat16)
    returned = lax.ppermute(away, "core", [(0, 1), (1, 0)])
    total = (down_project(h_own, sel_own, w[2]) + returned.astype(jnp.float32)).astype(jnp.bfloat16)
    for axis in GATHER_AXES[::-1]:
        total = lax.psum_scatter(total, axis, scatter_dimension=0, tiled=True)
    total = lax.psum_scatter(total.astype(jnp.float32), "z_hi", scatter_dimension=1, tiled=True)
    return lax.all_to_all(
        total.astype(jnp.bfloat16), "core", split_axis=1, concat_axis=0, tiled=True
    )


def solution(mesh):
    grid = Mesh(mesh.devices.reshape(4, 4, 4, 2, 2), ("y", "x", "z_lo", "z_hi", "core"))
    dp = ("z_hi", "core")
    return jax.shard_map(
        shards,
        mesh=grid,
        in_specs=(
            P(OWNER, None),
            P(OWNER, None, None, dp),
            P(),
            P(),
            P(OWNER, None),
            P(OWNER, None),
        ),
        out_specs=P(OWNER, dp),
        check_vma=False,
    )
```

profile of v0, /device:TPU:1, one launch (start us, length us, event | category | flops | bytes accessed | tf_op | source)
XLA Modules:
  0.0 520.1 jit_solution(11850227993452138166)
XLA Ops:
  6.5 0.7 convert_element_type.36
  7.4 0.8 copy.20
  8.1 1.1 concatenate.3
  9.2 18.9 %all_gather.9 = bf16[96,3712]{1,0:T(8,128)(2,1)} all-gather(bf16[24,3712]{1,0:T(8,128)(2,1)S(1)} %constant_dynamic-slice_fusion), channel_id=1, replica_groups=mesh['y'=4,'x'=4,'z_lo'=4,'z_hi'=2,'core'=2] {'z_lo'}, dimensions={0}, use_global_device_ids=true | all-gather | bytes 890880 | tf_op jit(solution)/shard_map/all_gather | solution.py:43
  28.2 42.4 %all-gather.3.cloned.1.call-done = bf16[384,3712]{1,0:T(8,128)(2,1)} async-done(((bf16[96,3712]{1,0:T(8,128)(2,1)}), bf16[384,3712]{1,0:T(8,128)(2,1)}) %all-gather.3.cloned.1.call-update) | async-done | bytes 2850832 | tf_op jit(solution)/shard_map/all_gather | solution.py:43
  70.8 113.1 %all-gather.5.cloned.1.call-done = bf16[1536,3712]{1,0:T(8,128)(2,1)} async-done(((bf16[384,3712]{1,0:T(8,128)(2,1)}), bf16[1536,3712]{1,0:T(8,128)(2,1)}) %all-gather.5.cloned.1.call-update) | async-done | bytes 11403280 | tf_op jit(solution)/shard_map/all_gather | solution.py:43
  183.8 0.7 collective-permute-start
  184.8 1.4 slice_convert_fusion.3
  186.2 15.7 %collective-permute-done = bf16[1536,3712]{1,0:T(8,128)(2,1)} collective-permute-done((bf16[1536,3712]{1,0:T(8,128)(2,1)}, bf16[1536,3712]{1,0:T(8,128)(2,1)}, u32[]{:S(2)}, u32[]{:S(2)}) %collective-permute-start) | collective-permute-done | bytes 11403296 | tf_op jit(solution)/shard_map/ppermute | solution.py:44
  202.0 1.3 slice_convert_fusion.1
  203.3 45.4 %select_reduce_fusion.1 = (f32[1536]{0:T(1024)S(1)}, f32[1536]{0:T(1024)S(1)}) fusion(f32[1536,8]{1,0:T(8,128)S(1)} %get-tuple-element.10, f32[1536,8]{1,0:T(8,128)S(1)} %get-tuple-element.9, pred[128]{0:T(512)(128)(4,1)S(1)} %eq.44, f32[1536,8]{1,0:T(8,128)S(1)} %get-tuple-element.8, f32[1536,8]{1,0:T(8,128)S(1)} %get-tuple-element.7), kind=kLoop, calls=%fused_computation.12 | loop fusion | flops 12579840 | bytes 209024 | tf_op jit(solution)/shard_map/reduce_sum | solution.py:15
  248.7 6.3 %fusion = f32[1536,256]{1,0:T(8,128)S(1)} fusion(bf16[1536,3712]{1,0:T(8,128)(2,1)} %collective-permute-done, bf16[1,3,3584,256]{3,2,1,0:T(8,128)(2,1)} %param.7), kind=kOutput, calls=%fused_computation.2 | convolution fusion | flops 2818572288 | bytes 14417920 | tf_op jit(solution)/shard_map/dot_general | solution.py:17
  255.0 17.7 %multiply_convert_fusion = bf16[1536,3584]{1,0:T(8,128)(2,1)} fusion(f32[1536]{0:T(1024)S(1)} %get-tuple-element.6, bf16[1,3,3584,256]{3,2,1,0:T(8,128)(2,1)} %param.7, f32[1536,256]{1,0:T(8,128)S(1)} %fusion, bf16[1536,3712]{1,0:T(8,128)(2,1)} %collective-permute-done), kind=kOutput, calls=%fused_computation.1 | convolution fusion | flops 5650513920 | bytes 27269120 | tf_op jit(solution)/shard_map/dot_general | solution.py:22
  272.7 0.4 collective-permute-start.1
  273.0 6.3 %fusion.6 = f32[1536,256]{1,0:T(8,128)S(1)} fusion(bf16[1536,3712]{1,0:T(8,128)(2,1)} %all-gather.5.cloned.1.call-done, bf16[1,3,3584,256]{3,2,1,0:T(8,128)(2,1)} %param.7), kind=kOutput, calls=%fused_computation.8 | convolution fusion | flops 2818572288 | bytes 14417920 | tf_op jit(solution)/shard_map/dot_general | solution.py:16
  279.4 10.5 %collective-permute-done.1 = bf16[1536,3584]{1,0:T(8,128)(2,1)} collective-permute-done((bf16[1536,3584]{1,0:T(8,128)(2,1)}, bf16[1536,3584]{1,0:T(8,128)(2,1)}, u32[]{:S(2)}, u32[]{:S(2)}) %collective-permute-start.1) | collective-permute-done | bytes 11010080 | tf_op jit(solution)/shard_map/ppermute | solution.py:50
  289.9 19.1 %add_convert_fusion = bf16[1536,3584]{1,0:T(8,128)(2,1)} fusion(bf16[1536,3584]{1,0:T(8,128)(2,1)} %collective-permute-done.1, f32[1536]{0:T(1024)S(1)} %get-tuple-element.5, bf16[1536,3712]{1,0:T(8,128)(2,1)} %all-gather.5.cloned.1.call-done, bf16[1,3,3584,256]{3,2,1,0:T(8,128)(2,1)} %param.7, f32[1536,256]{1,0:T(8,128)S(1)} %fusion.6), kind=kOutput, calls=%fused_computation | convolution fusion | flops 5661523968 | bytes 38279168 | tf_op jit(solution)/shard_map/dot_general | solution.py:22
  309.1 105.1 %reduce-scatter.5.cloned.1.call-done = bf16[384,3584]{1,0:T(8,128)(2,1)} async-done(((bf16[1536,3584]{1,0:T(8,128)(2,1)}), bf16[384,3584]{1,0:T(8,128)(2,1)}) %reduce-scatter.5.cloned.1.call-update) | async-done | bytes 2752528 | tf_op jit(solution)/shard_map/reduce_scatter | solution.py:53
  414.3 39.8 %reduce-scatter.7.cloned.1.call-done = bf16[96,3584]{1,0:T(8,128)(2,1)} async-done(((bf16[384,3584]{1,0:T(8,128)(2,1)}), bf16[96,3584]{1,0:T(8,128)(2,1)}) %reduce-scatter.7.cloned.1.call-update) | async-done | bytes 688144 | tf_op jit(solution)/shard_map/reduce_scatter | solution.py:53
  454.2 27.8 %reduce-scatter.9.cloned.1.call-done = bf16[24,3584]{1,0:T(8,128)(2,1)} async-done(((bf16[96,3584]{1,0:T(8,128)(2,1)}), bf16[24,3584]{1,0:T(8,128)(2,1)}) %reduce-scatter.9.cloned.1.call-update) | async-done | bytes 172048 | tf_op jit(solution)/shard_map/reduce_scatter | solution.py:53
  482.0 25.7 %reduce-scatter.11.cloned.1.call-done = bf16[24,1792]{1,0:T(8,128)(2,1)} async-done(((bf16[24,3584]{1,0:T(8,128)(2,1)}), bf16[24,1792]{1,0:T(8,128)(2,1)}) %reduce-scatter.11.cloned.1.call-update) | async-done | bytes 86032 | tf_op jit(solution)/shard_map/reduce_scatter | solution.py:54
  507.7 0.9 copy.25
  508.6 4.1 all_to_all.19
  512.7 0.6 copy.27
  (22 shorter events, 0.7 us)
Async XLA Ops:
  6.5 178.0 %copy-start.1 = (s32[64]{0:T(128)S(1)}, s32[64]{0:T(128)}, u32[]{:S(2)}) copy-start(s32[64]{0:T(128)} %param.8) | copy-start | bytes 772
  6.5 178.0 %copy-start = (s32[64]{0:T(128)S(1)}, s32[64]{0:T(128)}, u32[]{:S(2)}) copy-start(s32[64]{0:T(128)} %param.9) | copy-start | bytes 772
  6.5 64.1 %all-gather.3.cloned.1.call-start = ((), (), s32[]{:S(2)}) async-start(), calls=%async_computation.5 | async-start | bytes 3563520 | tf_op jit(solution)/shard_map/all_gather | solution.py:43
  28.2 155.6 %all-gather.5.cloned.1.call-start = ((), (), s32[]{:S(2)}) async-start(), calls=%async_computation.6 | async-start | bytes 14254080 | tf_op jit(solution)/shard_map/all_gather | solution.py:43
  70.7 343.6 %reduce-scatter.5.cloned.1.call-start = ((), (), s32[]{:S(2)}) async-start(), calls=%async_computation.7 | async-start | bytes 13762560 | tf_op jit(solution)/shard_map/reduce_scatter | solution.py:53
  183.8 18.1 %collective-permute-start = (bf16[1536,3712]{1,0:T(8,128)(2,1)}, bf16[1536,3712]{1,0:T(8,128)(2,1)}, u32[]{:S(2)}, u32[]{:S(2)}) collective-permute-start(bf16[1536,3712]{1,0:T(8,128)(2,1)} %all-gather.5.cloned.1.call-done), channel_id=1, source_target_pairs={{0,1},{1,0},{2,3},{3,2},{4,5},{5,4},{6,7},{7,6},{8,9},{9,8},{10,11... | collective-permute-start | bytes 34209800 | tf_op jit(solution)/shard_map/ppermute | solution.py:44
  272.7 17.2 %collective-permute-start.1 = (bf16[1536,3584]{1,0:T(8,128)(2,1)}, bf16[1536,3584]{1,0:T(8,128)(2,1)}, u32[]{:S(2)}, u32[]{:S(2)}) collective-permute-start(bf16[1536,3584]{1,0:T(8,128)(2,1)} %multiply_convert_fusion), channel_id=1, source_target_pairs={{0,1},{1,0},{2,3},{3,2},{4,5},{5,4},{6,7},{7,6},{8,9},{9,8},{10,11... | collective-permute-start | bytes 33030152 | tf_op jit(solution)/shard_map/ppermute | solution.py:50
  309.1 145.0 %reduce-scatter.7.cloned.1.call-start = ((), (), s32[]{:S(2)}) async-start(), calls=%async_computation.8 | async-start | bytes 3440640 | tf_op jit(solution)/shard_map/reduce_scatter | solution.py:53
  414.3 67.7 %reduce-scatter.9.cloned.1.call-start = ((), (), s32[]{:S(2)}) async-start(), calls=%async_computation.9 | async-start | bytes 860160 | tf_op jit(solution)/shard_map/reduce_scatter | solution.py:53
  454.1 53.6 %reduce-scatter.11.cloned.1.call-start = ((), (), s32[]{:S(2)}) async-start(), calls=%async_computation.10 | async-start | bytes 258048 | tf_op jit(solution)/shard_map/reduce_scatter | solution.py:54
Sparse Core Ops, SparseCore 0:
  28.3 42.3 all-gather.2
  72.5 111.2 all-gather.4
  309.2 105.0 reduce-scatter.4
  416.7 37.3 reduce-scatter.6
  456.5 25.4 reduce-scatter.8
  484.4 23.2 reduce-scatter.10
where the time goes:
time: 520 us
  waiting for transfers between devices  380 us (73%)
  matrix products  49.5 us (10%)
  other arithmetic  48.9 us (9%)
  blocking collectives  23 us (4%)
  between operations  13.5 us (3%)
    reduce_scatter x3, waiting for transfers between devices, shards(): total = lax.psum_scatter(total, axis, scatter_dimension=0, tiled=True)  173 us
    all_gather x2, waiting for transfers between devices, shards(): own = lax.all_gather(own, axis, axis=0, tiled=True)  156 us
    reduce_sum x1, other arithmetic, expert_hidden(): jnp.sum(jnp.where((slots[:, :, None] == ids) & hit, weight[:, :, None], 0...  45.4 us
    dot_general x2, matrix products, down_project(): lax.dot_general(h, w_down, (((1,), (1,)), ((), ())), preferred_element_ty...  36.8 us
    reduce_scatter x1, waiting for transfers between devices, shards(): lax.psum_scatter(total.astype(jnp.float32), 'z_hi', scatter_dimension=1,...  25.7 us
    all_gather x1, blocking collectives, shards(): own = lax.all_gather(own, axis, axis=0, tiled=True)  18.9 us
    ppermute x1, waiting for transfers between devices, shards(): other = lax.ppermute(own, 'core', [(0, 1), (1, 0)])  15.7 us
    ppermute x1, waiting for transfers between devices, shards(): returned = lax.ppermute(away, 'core', [(0, 1), (1, 0)])  10.5 us
  transfers between devices with their start and end apart: 8, of which 8 were waited for; matrix products, arithmetic and copies ran while one was open for 2% of the time, Pallas kernels for 0%

commit v1 on v0

--- a/solution.py
+++ b/solution.py
@@ -40,7 +40,9 @@
     )
     own = lax.dynamic_slice_in_dim(packed, core * half, half, axis=0)
     for axis in GATHER_AXES:
-        own = lax.all_gather(own, axis, axis=0, tiled=True)
+        own = jnp.concatenate(
+            lax.all_to_all(jnp.stack([own] * lax.axis_size(axis)), axis, 0, 0), axis=0
+        )
     other = lax.ppermute(own, "core", [(0, 1), (1, 0)])
     hit = jnp.stack([partner, replica], axis=1).reshape(-1) == me
     w = expert_weights[0]

time: 520 us -> 543 us (1.044)
  blocking collectives: 23 us -> 197 us
  waiting for transfers between devices: 380 us -> 220 us
    all_to_all x0 -> x3, blocking collectives: none -> 193 us  [shards(): lax.all_to_all(jnp.stack([own] * lax.axis_size(axis)), axis, 0, 0)]
    all_gather x2 -> x0, waiting for transfers between devices: 156 us -> none  [shards(): own = lax.all_gather(own, axis, axis=0, tiled=True)]
    all_gather x1 -> x0, blocking collectives: 18.9 us -> none  [shards(): own = lax.all_gather(own, axis, axis=0, tiled=True)]
  transfers between devices with their start and end apart: 8 -> 6, of which waited for: 8 -> 6; matrix products, arithmetic and copies ran while one was open for 2% -> 1% of each run, Pallas kernels for 0% -> 0%
where the time goes in v1:
time: 543 us; the launch traced here: 542 us
  waiting for transfers between devices  220 us (41%)
  blocking collectives  197 us (36%)
  matrix products  49.5 us (9%)
  other arithmetic  48.9 us (9%)
  between operations  13.2 us (2%)
  local copies, waits for them, and re-layouts  8.95 us (2%)
    all_to_all x3, blocking collectives, shards(): lax.all_to_all(jnp.stack([own] * lax.axis_size(axis)), axis, 0, 0)  193 us
    reduce_scatter x3, waiting for transfers between devices, shards(): total = lax.psum_scatter(total, axis, scatter_dimension=0, tiled=True)  168 us
    reduce_sum x1, other arithmetic, expert_hidden(): jnp.sum(jnp.where((slots[:, :, None] == ids) & hit, weight[:, :, None], 0...  45.4 us
    dot_general x2, matrix products, down_project(): lax.dot_general(h, w_down, (((1,), (1,)), ((), ())), preferred_element_ty...  36.8 us
    reduce_scatter x1, waiting for transfers between devices, shards(): lax.psum_scatter(total.astype(jnp.float32), 'z_hi', scatter_dimension=1,...  26 us
    ppermute x1, waiting for transfers between devices, shards(): other = lax.ppermute(own, 'core', [(0, 1), (1, 0)])  15.6 us
  transfers between devices with their start and end apart: 6, of which 6 were waited for; matrix products, arithmetic and copies ran while one was open for 1% of the time, Pallas kernels for 0%

profile of v1, /device:TPU:1, one launch (start us, length us, event | category | flops | bytes accessed | tf_op | source)
XLA Modules:
  0.0 542.0 jit_solution(10374392510119692293)
XLA Ops:
  6.5 0.7 convert_element_type.36
  7.3 0.8 copy.20
  8.1 1.1 concatenate.3
  9.3 24.2 %all_to_all.34 = bf16[4,24,3712]{2,1,0:T(8,128)(2,1)S(1)} all-to-all(bf16[4,24,3712]{2,1,0:T(8,128)(2,1)S(1)} %stack.22), channel_id=1, replica_groups=mesh['y'=4,'x'=4,'z_lo'=4,'z_hi'=2,'core'=2] {'z_lo'}, dimensions={0} | all-to-all | bytes 1425408 | tf_op jit(solution)/shard_map/all_to_all | solution.py:44
  33.7 36.3 %all_to_all.35 = bf16[4,96,3712]{2,1,0:T(8,128)(2,1)S(1)} all-to-all(bf16[4,96,3712]{2,1,0:T(8,128)(2,1)S(1)} %stack.23), channel_id=1, replica_groups=mesh['y'=4,'x'=4,'z_lo'=4,'z_hi'=2,'core'=2] {'y'}, dimensions={0} | all-to-all | bytes 5701632 | tf_op jit(solution)/shard_map/all_to_all | solution.py:44
  70.0 4.9 stack.24
  75.0 132.1 %all_to_all.36 = bf16[4,384,3712]{2,1,0:T(8,128)(2,1)} all-to-all(bf16[4,384,3712]{2,1,0:T(8,128)(2,1)} %stack.24), channel_id=1, replica_groups=mesh['y'=4,'x'=4,'z_lo'=4,'z_hi'=2,'core'=2] {'x'}, dimensions={0} | all-to-all | bytes 22806528 | tf_op jit(solution)/shard_map/all_to_all | solution.py:44
  207.1 3.9 collective-permute-start
  211.3 1.5 slice_convert_fusion.3
  212.8 15.6 %collective-permute-done = bf16[1536,3712]{1,0:T(8,128)(2,1)} collective-permute-done((bf16[1536,3712]{1,0:T(8,128)(2,1)}, bf16[1536,3712]{1,0:T(8,128)(2,1)}, u32[]{:S(2)}, u32[]{:S(2)}) %collective-permute-start) | collective-permute-done | bytes 11403296 | tf_op jit(solution)/shard_map/ppermute | solution.py:46
  228.4 1.3 slice_convert_fusion.1
  229.8 45.4 %select_reduce_fusion.1 = (f32[1536]{0:T(1024)S(1)}, f32[1536]{0:T(1024)S(1)}) fusion(f32[1536,8]{1,0:T(8,128)S(1)} %get-tuple-element.10, f32[1536,8]{1,0:T(8,128)S(1)} %get-tuple-element.9, pred[128]{0:T(512)(128)(4,1)S(1)} %eq.44, f32[1536,8]{1,0:T(8,128)S(1)} %get-tuple-element.8, f32[1536,8]{1,0:T(8,128)S(1)} %get-tuple-element.7), kind=kLoop, calls=%fused_computation.12 | loop fusion | flops 12579840 | bytes 209024 | tf_op jit(solution)/shard_map/reduce_sum | solution.py:15
  275.1 6.3 %fusion = f32[1536,256]{1,0:T(8,128)S(1)} fusion(bf16[1536,3712]{1,0:T(8,128)(2,1)} %collective-permute-done, bf16[1,3,3584,256]{3,2,1,0:T(8,128)(2,1)} %param.7), kind=kOutput, calls=%fused_computation.2 | convolution fusion | flops 2818572288 | bytes 14417920 | tf_op jit(solution)/shard_map/dot_general | solution.py:17
  281.5 17.6 %multiply_convert_fusion = bf16[1536,3584]{1,0:T(8,128)(2,1)} fusion(f32[1536]{0:T(1024)S(1)} %get-tuple-element.6, bf16[1,3,3584,256]{3,2,1,0:T(8,128)(2,1)} %param.7, f32[1536,256]{1,0:T(8,128)S(1)} %fusion, bf16[1536,3712]{1,0:T(8,128)(2,1)} %collective-permute-done), kind=kOutput, calls=%fused_computation.1 | convolution fusion | flops 5650513920 | bytes 27269120 | tf_op jit(solution)/shard_map/dot_general | solution.py:22
  299.5 6.3 %fusion.6 = f32[1536,256]{1,0:T(8,128)S(1)} fusion(bf16[1536,3712]{1,0:T(8,128)(2,1)} %bitcast.2, bf16[1,3,3584,256]{3,2,1,0:T(8,128)(2,1)} %param.7), kind=kOutput, calls=%fused_computation.8 | convolution fusion | flops 2818572288 | bytes 14417920 | tf_op jit(solution)/shard_map/dot_general | solution.py:16
  305.8 10.5 %collective-permute-done.1 = bf16[1536,3584]{1,0:T(8,128)(2,1)} collective-permute-done((bf16[1536,3584]{1,0:T(8,128)(2,1)}, bf16[1536,3584]{1,0:T(8,128)(2,1)}, u32[]{:S(2)}, u32[]{:S(2)}) %collective-permute-start.1) | collective-permute-done | bytes 11010080 | tf_op jit(solution)/shard_map/ppermute | solution.py:52
  316.4 19.1 %add_convert_fusion = bf16[1536,3584]{1,0:T(8,128)(2,1)} fusion(bf16[1536,3584]{1,0:T(8,128)(2,1)} %collective-permute-done.1, f32[1536]{0:T(1024)S(1)} %get-tuple-element.5, bf16[1536,3712]{1,0:T(8,128)(2,1)} %bitcast.2, bf16[1,3,3584,256]{3,2,1,0:T(8,128)(2,1)} %param.7, f32[1536,256]{1,0:T(8,128)S(1)} %fusion.6), kind=kOutput, calls=%fused_computation | convolution fusion | flops 5661523968 | bytes 38279168 | tf_op jit(solution)/shard_map/dot_general | solution.py:22
  335.6 100.5 %reduce-scatter.5.cloned.1.call-done = bf16[384,3584]{1,0:T(8,128)(2,1)} async-done(((bf16[1536,3584]{1,0:T(8,128)(2,1)}), bf16[384,3584]{1,0:T(8,128)(2,1)}) %reduce-scatter.5.cloned.1.call-update) | async-done | bytes 2752528 | tf_op jit(solution)/shard_map/reduce_scatter | solution.py:55
  436.2 39.9 %reduce-scatter.7.cloned.1.call-done = bf16[96,3584]{1,0:T(8,128)(2,1)} async-done(((bf16[384,3584]{1,0:T(8,128)(2,1)}), bf16[96,3584]{1,0:T(8,128)(2,1)}) %reduce-scatter.7.cloned.1.call-update) | async-done | bytes 688144 | tf_op jit(solution)/shard_map/reduce_scatter | solution.py:55
  476.2 27.7 %reduce-scatter.9.cloned.1.call-done = bf16[24,3584]{1,0:T(8,128)(2,1)} async-done(((bf16[96,3584]{1,0:T(8,128)(2,1)}), bf16[24,3584]{1,0:T(8,128)(2,1)}) %reduce-scatter.9.cloned.1.call-update) | async-done | bytes 172048 | tf_op jit(solution)/shard_map/reduce_scatter | solution.py:55
  503.8 26.0 %reduce-scatter.11.cloned.1.call-done = bf16[24,1792]{1,0:T(8,128)(2,1)} async-done(((bf16[24,3584]{1,0:T(8,128)(2,1)}), bf16[24,1792]{1,0:T(8,128)(2,1)}) %reduce-scatter.11.cloned.1.call-update) | async-done | bytes 86032 | tf_op jit(solution)/shard_map/reduce_scatter | solution.py:56
  529.9 0.9 copy.25
  530.8 4.1 all_to_all.37
  534.8 0.6 copy.27
  (21 shorter events, 1.2 us)
Async XLA Ops:
  6.5 429.6 %reduce-scatter.5.cloned.1.call-start = ((), (), s32[]{:S(2)}) async-start(), calls=%async_computation.8 | async-start | bytes 13762560 | tf_op jit(solution)/shard_map/reduce_scatter | solution.py:55
  74.9 136.1 %copy-start = (s32[64]{0:T(128)S(1)}, s32[64]{0:T(128)}, u32[]{:S(2)}) copy-start(s32[64]{0:T(128)} %param.9) | copy-start | bytes 772
  74.9 136.1 %copy-start.1 = (s32[64]{0:T(128)S(1)}, s32[64]{0:T(128)}, u32[]{:S(2)}) copy-start(s32[64]{0:T(128)} %param.8) | copy-start | bytes 772
  207.1 21.4 %collective-permute-start = (bf16[1536,3712]{1,0:T(8,128)(2,1)}, bf16[1536,3712]{1,0:T(8,128)(2,1)}, u32[]{:S(2)}, u32[]{:S(2)}) collective-permute-start(bf16[1536,3712]{1,0:T(8,128)(2,1)} %bitcast.2), channel_id=1, source_target_pairs={{0,1},{1,0},{2,3},{3,2},{4,5},{5,4},{6,7},{7,6},{8,9},{9,8},{10,11... | collective-permute-start | bytes 34209800 | tf_op jit(solution)/shard_map/ppermute | solution.py:46
  299.1 17.2 %collective-permute-start.1 = (bf16[1536,3584]{1,0:T(8,128)(2,1)}, bf16[1536,3584]{1,0:T(8,128)(2,1)}, u32[]{:S(2)}, u32[]{:S(2)}) collective-permute-start(bf16[1536,3584]{1,0:T(8,128)(2,1)} %multiply_convert_fusion), channel_id=1, source_target_pairs={{0,1},{1,0},{2,3},{3,2},{4,5},{5,4},{6,7},{7,6},{8,9},{9,8},{10,11... | collective-permute-start | bytes 33030152 | tf_op jit(solution)/shard_map/ppermute | solution.py:52
  335.6 140.5 %reduce-scatter.7.cloned.1.call-start = ((), (), s32[]{:S(2)}) async-start(), calls=%async_computation.9 | async-start | bytes 3440640 | tf_op jit(solution)/shard_map/reduce_scatter | solution.py:55
  436.1 67.7 %reduce-scatter.9.cloned.1.call-start = ((), (), s32[]{:S(2)}) async-start(), calls=%async_computation.10 | async-start | bytes 860160 | tf_op jit(solution)/shard_map/reduce_scatter | solution.py:55
  476.1 53.8 %reduce-scatter.11.cloned.1.call-start = ((), (), s32[]{:S(2)}) async-start(), calls=%async_computation.11 | async-start | bytes 258048 | tf_op jit(solution)/shard_map/reduce_scatter | solution.py:56
Sparse Core Ops, SparseCore 0:
  335.7 100.3 reduce-scatter.4
  438.7 37.3 reduce-scatter.6
  478.6 25.1 reduce-scatter.8
  506.3 23.5 reduce-scatter.10
